TPU v7x, 32 devices: a whole 2x2x4 slice. The times are simulated.
32 devices in a mesh: dp: 16 (over z, y, core), seq: 2 (over x).
Axes of the slice: x: 2, y: 2, z: 4, core: 2. Of those that a mesh axis runs over, the one named last changes fastest.
Arguments:
- tokens: bfloat16 [16, 1024, 1024], P('dp', 'seq'), may hold values from -6 to 6
- cotangent: bfloat16 [16, 1024, 1024], P('dp', 'seq'), may hold values from -6 to 6
- doc_lengths: int32 [16, 8], P('dp'), may hold values from 1 to 512, 1024 in all within a row
- attn_gain: bfloat16 [1024], replicated, may hold values from 0.5 to 1.5
- w_query: bfloat16 [1024, 1024], replicated, may hold values from -0.1875 to 0.1875
- w_key: bfloat16 [1024, 512], replicated, may hold values from -0.1875 to 0.1875
- w_value: bfloat16 [1024, 512], replicated, may hold values from -0.1875 to 0.1875
- query_gain: bfloat16 [64], replicated, may hold values from 0.5 to 1.5
- key_gain: bfloat16 [64], replicated, may hold values from 0.5 to 1.5
- w_out: bfloat16 [1024, 1024], replicated, may hold values from -3 to 3
- ffn_gain: bfloat16 [1024], replicated, may hold values from 0.5 to 1.5
- w_gate: bfloat16 [1024, 4608], replicated, may hold values from -0.1875 to 0.1875
- w_up: bfloat16 [1024, 4608], replicated, may hold values from -0.1875 to 0.1875
- w_down: bfloat16 [4608, 1024], replicated, may hold values from -0.09375 to 0.09375
Outputs:
- output: float32 [16, 1024, 1024], P('dp', 'seq')
- d_tokens: float32 [16, 1024, 1024], P('dp', 'seq')
- d_attn_gain: float32 [1024], replicated
- d_w_query: float32 [1024, 1024], P('dp', 'seq')
- d_w_key: float32 [1024, 512], P('dp', 'seq')
- d_w_value: float32 [1024, 512], P('dp', 'seq')
- d_query_gain: float32 [64], replicated
- d_key_gain: float32 [64], replicated
- d_w_out: float32 [1024, 1024], P('dp', 'seq')
- d_ffn_gain: float32 [1024], replicated
- d_w_gate: float32 [1024, 4608], P('dp', 'seq')
- d_w_up: float32 [1024, 4608], P('dp', 'seq')
- d_w_down: float32 [4608, 1024], P('dp', 'seq')
Inputs may be any that keep to these rules, and one draw needn't show every extreme that they name: `doc_lengths`: each row's 8 documents fill its 1024 positions, and one of them is 512 long.
All inputs are finite; a program needn't handle non-finite values.
Results may differ from a plain program's by a relative error of at most 0.014.
Values may be sent and summed in bfloat16 or wider, within the bound.
No kernel may reach another device: no remote copies, remote signals or barrier semaphores. Data moves between devices by JAX's collectives and lax.ppermute only.
A program may use at most 256 MiB of HBM per device.

v0:
```python
import math
import jax
import jax.numpy as jnp
from jax import lax
from jax.sharding import PartitionSpec as P

EPSILON = 1e-06


def rms_scale(values, gain):
    return values * lax.rsqrt(jnp.mean(values * values, axis=-1, keepdims=True) + EPSILON) * gain


def norm_back(incoming, values, gain):
    inverse = lax.rsqrt(jnp.mean(values * values, axis=-1, keepdims=True) + EPSILON)
    unit = values * inverse
    scaled = incoming * gain
    d_values = inverse * (scaled - unit * jnp.mean(scaled * unit, axis=-1, keepdims=True))
    return (d_values, incoming * unit)


def rope_tables(first, count, width):
    half = width // 2
    spread = jnp.exp(jnp.arange(half, dtype=jnp.float32) * (-2.0 * math.log(1000000.0) / width))
    places = (first + jnp.arange(count, dtype=jnp.int32)).astype(jnp.float32)
    angles = places[:, None] * spread[None, :]
    return (jnp.cos(angles)[:, None, :], jnp.sin(angles)[:, None, :])


def rotate(values, cosine, sine):
    half = values.shape[-1] // 2
    first_half = values[..., :half]
    second_half = values[..., half:]
    return jnp.concatenate(
        [first_half * cosine - second_half * sine, second_half * cosine + first_half * sine],
        axis=-1,
    )


def reduce_grads(grads):
    partial_sum = lax.psum_scatter(grads, "dp", scatter_dimension=0, tiled=True)
    return lax.psum_scatter(partial_sum, "seq", scatter_dimension=1, tiled=True)


def body(
    tokens,
    cotangent,
    doc_lengths,
    attn_gain,
    w_query,
    w_key,
    w_value,
    query_gain,
    key_gain,
    w_out,
    ffn_gain,
    w_gate,
    w_up,
    w_down,
):
    shards = lax.axis_size("seq")
    local = tokens.shape[1]
    length = local * shards
    head_size = query_gain.shape[0]
    kv_count = w_key.shape[1] // head_size
    head_count = w_query.shape[1] // head_size
    group = head_count // kv_count
    kv_local = kv_count // shards
    block = min(512, length)
    num_blocks = length // block
    scale = head_size ** (-0.5)
    f32 = jnp.float32
    bf16 = jnp.bfloat16
    gain_attn = attn_gain.astype(f32)
    gain_query = query_gain.astype(f32)
    gain_key = key_gain.astype(f32)
    gain_ffn = ffn_gain.astype(f32)
    inputs = tokens[0].astype(f32)
    normed = rms_scale(inputs, gain_attn).astype(bf16)
    query_raw = jnp.dot(normed, w_query, preferred_element_type=f32).reshape(
        local, head_count, head_size
    )
    key_raw = jnp.dot(normed, w_key, preferred_element_type=f32).reshape(local, kv_count, head_size)
    values = (
        jnp.dot(normed, w_value, preferred_element_type=f32)
        .astype(bf16)
        .reshape(local, kv_count, head_size)
    )
    cosine, sine = rope_tables(lax.axis_index("seq") * local, local, head_size)
    query_rot = rotate(rms_scale(query_raw, gain_query), cosine, sine).astype(bf16)
    key_rot = rotate(rms_scale(key_raw, gain_key), cosine, sine).astype(bf16)
    packed_query = query_rot.reshape(local, kv_count, group * head_size)
    packed_kv = jnp.concatenate([key_rot, values], axis=2)
    query_heads, kv_heads = (
        lax.all_to_all(packed_query, "seq", split_axis=1, concat_axis=0, tiled=True),
        lax.all_to_all(packed_kv, "seq", split_axis=1, concat_axis=0, tiled=True),
    )
    query_all = query_heads.reshape(length, kv_local, group, head_size)
    key_all = kv_heads[:, :, :head_size]
    value_all = kv_heads[:, :, head_size:]
    positions = jnp.arange(length, dtype=jnp.int32)
    ends = jnp.cumsum(doc_lengths[0])
    segment = jnp.sum((ends[None, :] <= positions[:, None]).astype(jnp.int32), axis=1)
    starts = jnp.arange(num_blocks, dtype=jnp.int32) * block

    def allowed_at(begin):
        rows_here = begin + jnp.arange(block, dtype=jnp.int32)
        query_seg = lax.dynamic_slice_in_dim(segment, begin, block, 0)
        return (query_seg[:, None] == segment[None, :]) & (positions[None, :] <= rows_here[:, None])

    def block_scores(begin):
        query_block = lax.dynamic_slice_in_dim(query_all, begin, block, 0)
        scores = (
            jnp.einsum("qhgd,khd->hgqk", query_block, key_all, preferred_element_type=f32) * scale
        )
        return (query_block, jnp.where(allowed_at(begin), scores, -jnp.inf))

    def attend(begin):
        query_block, scores = block_scores(begin)
        top_score = jnp.max(scores, axis=-1, keepdims=True)
        expos = jnp.exp(scores - top_score)
        totals = jnp.sum(expos, axis=-1, keepdims=True)
        probs = (expos / totals).astype(bf16)
        result = jnp.einsum("hgqk,khd->qhgd", probs, value_all, preferred_element_type=f32)
        return (result.astype(bf16), top_score[..., 0] + jnp.log(totals[..., 0]))

    attended_heads, log_totals = lax.map(attend, starts)
    attended_heads = attended_heads.reshape(length, kv_local, group * head_size)
    attended = lax.all_to_all(
        attended_heads, "seq", split_axis=0, concat_axis=1, tiled=True
    ).reshape(local, head_count * head_size)
    hidden = inputs + jnp.dot(attended, w_out, preferred_element_type=f32)
    hnormed = rms_scale(hidden, gain_ffn).astype(bf16)
    gate = jnp.dot(hnormed, w_gate, preferred_element_type=f32)
    up_part = jnp.dot(hnormed, w_up, preferred_element_type=f32)
    act = (jax.nn.silu(gate) * up_part).astype(bf16)
    output = hidden + jnp.dot(act, w_down, preferred_element_type=f32)
    d_mlp = cotangent[0]
    grad_down = jnp.einsum("tf,td->fd", act, d_mlp, preferred_element_type=f32)
    d_act = jnp.einsum("td,fd->tf", d_mlp, w_down, preferred_element_type=f32)
    gate_again = jnp.dot(hnormed, w_gate, preferred_element_type=f32)
    up_again = jnp.dot(hnormed, w_up, preferred_element_type=f32)
    sigmoid_gate = jax.nn.sigmoid(gate_again)
    d_up = (d_act * gate_again * sigmoid_gate).astype(bf16)
    d_gate = (d_act * up_again * sigmoid_gate * (1.0 + gate_again * (1.0 - sigmoid_gate))).astype(
        bf16
    )
    grad_gate = jnp.einsum("td,tf->df", hnormed, d_gate, preferred_element_type=f32)
    grad_up = jnp.einsum("td,tf->df", hnormed, d_up, preferred_element_type=f32)
    ffn_sums = reduce_grads((grad_gate, grad_up, grad_down))
    d_hnormed = jnp.einsum("tf,df->td", d_gate, w_gate, preferred_element_type=f32) + jnp.einsum(
        "tf,df->td", d_up, w_up, preferred_element_type=f32
    )
    d_hidden_norm, ffn_gain_terms = norm_back(d_hnormed, hidden, gain_ffn)
    d_hidden = cotangent[0].astype(f32) + d_hidden_norm
    d_attn = d_hidden.astype(bf16)
    grad_out = jnp.einsum("tf,td->fd", attended, d_attn, preferred_element_type=f32)
    d_attended = jnp.einsum("td,fd->tf", d_attn, w_out, preferred_element_type=f32).astype(bf16)
    d_heads = lax.all_to_all(
        d_attended.reshape(local, kv_count, group * head_size),
        "seq",
        split_axis=1,
        concat_axis=0,
        tiled=True,
    )
    d_all = d_heads.reshape(length, kv_local, group, head_size)

    def attend_back(carry, item):
        begin, log_block = item
        query_block, scores = block_scores(begin)
        probs = jnp.exp(scores - log_block[..., None])
        d_block = lax.dynamic_slice_in_dim(d_all, begin, block, 0)
        d_probs = jnp.einsum("qhgd,khd->hgqk", d_block, value_all, preferred_element_type=f32)
        delta = jnp.sum(probs * d_probs, axis=-1, keepdims=True)
        d_scores = (scale * (probs * (d_probs - delta))).astype(bf16)
        d_query_block = jnp.einsum("hgqk,khd->qhgd", d_scores, key_all, preferred_element_type=f32)
        key_total = carry[0] + jnp.einsum(
            "hgqk,qhgd->khd", d_scores, query_block, preferred_element_type=f32
        )
        value_total = carry[1] + jnp.einsum(
            "hgqk,qhgd->khd", probs.astype(bf16), d_block, preferred_element_type=f32
        )
        return ((key_total, value_total), d_query_block.astype(bf16))

    empty = jnp.zeros((length, kv_local, head_size), f32)
    (d_keys, d_values), d_queries = lax.scan(attend_back, (empty, empty), (starts, log_totals))
    d_queries = d_queries.reshape(length, kv_local, group * head_size)
    d_kv = jnp.concatenate([d_keys.astype(bf16), d_values.astype(bf16)], axis=2)
    d_query_pos, d_kv_pos = (
        lax.all_to_all(d_queries, "seq", split_axis=0, concat_axis=1, tiled=True),
        lax.all_to_all(d_kv, "seq", split_axis=0, concat_axis=1, tiled=True),
    )
    d_query_rot = d_query_pos.reshape(local, head_count, head_size).astype(f32)
    d_query_raw, query_gain_terms = norm_back(
        rotate(d_query_rot, cosine, -sine), query_raw, gain_query
    )
    d_query_low = d_query_raw.reshape(local, head_count * head_size).astype(bf16)
    d_key_rot = d_kv_pos[:, :, :head_size].astype(f32)
    d_key_raw, key_gain_terms = norm_back(rotate(d_key_rot, cosine, -sine), key_raw, gain_key)
    d_key_low = d_key_raw.reshape(local, kv_count * head_size).astype(bf16)
    d_value_low = d_kv_pos[:, :, head_size:].reshape(local, kv_count * head_size)
    grad_query = jnp.einsum("td,tf->df", normed, d_query_low, preferred_element_type=f32)
    grad_key = jnp.einsum("td,tf->df", normed, d_key_low, preferred_element_type=f32)
    grad_value = jnp.einsum("td,tf->df", normed, d_value_low, preferred_element_type=f32)
    d_normed = jnp.einsum("tf,df->td", d_query_low, w_query, preferred_element_type=f32)
    d_normed = d_normed + jnp.einsum("tf,df->td", d_key_low, w_key, preferred_element_type=f32)
    d_normed = d_normed + jnp.einsum("tf,df->td", d_value_low, w_value, preferred_element_type=f32)
    d_input_norm, attn_gain_terms = norm_back(d_normed, inputs, gain_attn)
    d_inputs = d_hidden + d_input_norm
    attn_sums = reduce_grads((grad_query, grad_key, grad_value, grad_out))
    gain_totals = lax.psum(
        (
            jnp.sum(attn_gain_terms, axis=0),
            jnp.sum(query_gain_terms, axis=(0, 1)),
            jnp.sum(key_gain_terms, axis=(0, 1)),
            jnp.sum(ffn_gain_terms, axis=0),
        ),
        ("dp", "seq"),
    )
    return (
        output[None],
        d_inputs[None],
        gain_totals[0],
        attn_sums[0],
        attn_sums[1],
        attn_sums[2],
        gain_totals[1],
        gain_totals[2],
        attn_sums[3],
        gain_totals[3],
        ffn_sums[0],
        ffn_sums[1],
        ffn_sums[2],
    )


def solution(mesh):
    return jax.shard_map(
        body,
        mesh=mesh,
        in_specs=(
            P("dp", "seq", None),
            P("dp", "seq", None),
            P("dp", None),
            P(),
            P(),
            P(),
            P(),
            P(),
            P(),
            P(),
            P(),
            P(),
            P(),
            P(),
        ),
        out_specs=(
            P("dp", "seq", None),
            P("dp", "seq", None),
            P(),
            P("dp", "seq"),
            P("dp", "seq"),
            P("dp", "seq"),
            P(),
            P(),
            P("dp", "seq"),
            P(),
            P("dp", "seq"),
            P("dp", "seq"),
            P("dp", "seq"),
        ),
        check_vma=False,
    )
```

profile of v0, /device:TPU:0, one launch (start us, length us, event | category | flops | bytes accessed | tf_op | source)
XLA Modules:
  0.0 1398.1 jit_solution(11515140757117083535)
XLA Ops:
  19.7 4.4 all-to-all-start.1
  33.7 5.5 all-to-all-done.1
  39.2 4.6 all-to-all-start
  49.3 7.9 all-to-all-done
  64.2 36.4 %while.28 = (s32[]{:T(128)}, bf16[2,512,4,2,64]{1,4,3,2,0:T(8,128)(2,1)}, f32[2,4,2,512]{3,2,1,0:T(2,128)S(1)}, s32[2]{0:T(128)S(1)}, s32[1024]{0:T(1024)S(1)}, ...) while((s32[]{:T(128)}, ...), condition=%wide.region_8.9_spmd.clone, body=%wide.region_5.8_spmd.clone.sunk | while | flops 1125904896 | bytes 54672044 | solution.py:127
  68.0 4.4 bitcast_reduce_fusion.2
  76.8 5.6 fusion.162
  86.2 4.4 bitcast_reduce_fusion.2
  95.0 5.6 fusion.162
  100.6 6.1 copy.115
  106.7 5.1 reshape.352
  111.8 4.9 all-to-all-start.2
  116.7 12.4 all-to-all-done.2
  138.4 7.6 fusion.102
  146.0 7.4 fusion.103
  153.4 20.4 %multiply_convert_fusion = (bf16[512,4608]{1,0:T(8,128)(2,1)}, bf16[512,4608]{1,0:T(8,128)(2,1)}, bf16[512,4608]{1,0:T(8,128)(2,1)}) fusion(f32[512,4608]{1,0:T(8,128)} %fusion.102, f32[512,4608]{1,0:T(8,128)} %fusion.103, bf16[4608,1024]{1,0:T(8,128)(2,1)} %param.31, bf16[1,512,1024]{2,1,0:T(8,128)(2,1)S(1)} %copy-done.27), kind=kOutput, calls=%fused_computation.63 | convolution fusion | flops 4869586944 | bytes 43515904 | tf_op jit(solution)/shard_map/td,fd->tf/dot_general | solution.py:140
  173.8 9.2 fusion.104
  183.0 8.8 multiply_reduce_fusion
  198.6 11.4 all-to-all-done.3
  215.0 155.5 %while.29 = (s32[]{:T(128)}, f32[1024,4,64]{0,2,1:T(8,128)}, f32[1024,4,64]{0,2,1:T(8,128)S(1)}, bf16[2,512,4,2,64]{1,4,3,2,0:T(8,128)(2,1)}, s32[2]{0:T(128)S(1...) while((s32[]{:T(128)}, f32[1024,4,64]{0,2,1:T(8,128)}, ...), condition=%wide.region_13.14_spmd.clone, body=%wide.region_11.13_spmd.clone.sunk | while | flops 2745969152 | bytes 194050784 | solution.py:186
  218.8 9.6 fusion.172
  228.4 8.2 fusion.173
  236.6 25.5 %fusion.176 = bf16[2,512,4,2,64]{1,4,3,2,0:T(8,128)(2,1)} fusion(bf16[2,512,4,2,64]{1,4,3,2,0:T(8,128)(2,1)} %get-tuple-element.434, s32[]{:T(128)} %get-tuple-element.431, f32[4,2,512,1024]{3,2,1,0:T(8,128)} %fusion.172, f32[4,512,2,1024]{3,1,2,0:T(8,128)} %fusion.173, bf16[1024,4,64]{0,2,1:T(8,128)(2,1)S(1)} %get-tuple-element.452), kind=kOutput, calls=%fused_computation.44.clone.1 | convolution fusion | flops 558109696 | bytes 68157952 | tf_op jit(solution)/shard_map/while/body/eval_jaxpr/hgqk,khd->qhgd/dot_general | solution.py:176
  262.1 22.9 %fusion.174 = f32[1024,4,64]{0,2,1:T(8,128)} fusion(f32[4,2,512,1024]{3,2,1,0:T(8,128)} %fusion.172, f32[4,512,2,1024]{3,1,2,0:T(8,128)} %fusion.173, f32[1024,4,64]{0,2,1:T(8,128)} %get-tuple-element.432, pred[]{:T(512)S(6)} %compare.3, bf16[1024,4,2,64]{0,3,2,1:T(8,128)(2,1)} %get-tuple-element.450, s32[]{:T(128)S(6)} %select_n.56), kind=kOutput, calls=%fused_computation.39.clone.1 | convolution fusion | flops 558371840 | bytes 69730312 | tf_op jit(solution)/shard_map/while/body/eval_jaxpr/hgqk,qhgd->khd/dot_general | solution.py:177
  284.9 7.6 fusion.175
  296.4 9.6 fusion.172
  306.0 8.2 fusion.173
  314.2 25.5 %fusion.176 = bf16[2,512,4,2,64]{1,4,3,2,0:T(8,128)(2,1)} fusion(bf16[2,512,4,2,64]{1,4,3,2,0:T(8,128)(2,1)} %get-tuple-element.434, s32[]{:T(128)} %get-tuple-element.431, f32[4,2,512,1024]{3,2,1,0:T(8,128)} %fusion.172, f32[4,512,2,1024]{3,1,2,0:T(8,128)} %fusion.173, bf16[1024,4,64]{0,2,1:T(8,128)(2,1)S(1)} %get-tuple-element.452), kind=kOutput, calls=%fused_computation.44.clone.1 | convolution fusion | flops 558109696 | bytes 68157952 | tf_op jit(solution)/shard_map/while/body/eval_jaxpr/hgqk,khd->qhgd/dot_general | solution.py:176
  339.7 23.2 %fusion.174 = f32[1024,4,64]{0,2,1:T(8,128)} fusion(f32[4,2,512,1024]{3,2,1,0:T(8,128)} %fusion.172, f32[4,512,2,1024]{3,1,2,0:T(8,128)} %fusion.173, f32[1024,4,64]{0,2,1:T(8,128)} %get-tuple-element.432, pred[]{:T(512)S(6)} %compare.3, bf16[1024,4,2,64]{0,3,2,1:T(8,128)(2,1)} %get-tuple-element.450, s32[]{:T(128)S(6)} %select_n.56), kind=kOutput, calls=%fused_computation.39.clone.1 | convolution fusion | flops 558371840 | bytes 69730312 | tf_op jit(solution)/shard_map/while/body/eval_jaxpr/hgqk,qhgd->khd/dot_general | solution.py:177
  362.8 7.6 fusion.175
  372.6 13.2 all_to_all.90
  395.1 4.5 fusion.91
  399.8 4.6 copy.116
  406.1 13.2 all_to_all.91
  430.9 11.6 fusion.107
  442.6 11.8 fusion.108
  455.6 11.7 fusion.75
  468.1 49.3 %reduce-scatter.23.cloned.1.call-done = f32[64,512]{1,0:T(8,128)} async-done(((f32[1024,512]{1,0:T(8,128)}), f32[64,512]{1,0:T(8,128)}) %reduce-scatter.23.cloned.1.call-update) | async-done | bytes 131088 | tf_op jit(solution)/shard_map/reduce_scatter | solution.py:41
  517.4 75.6 %reduce-scatter.27.cloned.1.call-done = f32[64,1024]{1,0:T(8,128)} async-done(((f32[1024,1024]{1,0:T(8,128)}), f32[64,1024]{1,0:T(8,128)}) %reduce-scatter.27.cloned.1.call-update) | async-done | bytes 262160 | tf_op jit(solution)/shard_map/reduce_scatter | solution.py:41
  593.1 75.9 %reduce-scatter.15.cloned.1.call-done = f32[64,1024]{1,0:T(8,128)} async-done(((f32[1024,1024]{1,0:T(8,128)}), f32[64,1024]{1,0:T(8,128)}) %reduce-scatter.15.cloned.1.call-update) | async-done | bytes 262160 | tf_op jit(solution)/shard_map/reduce_scatter | solution.py:41
  669.1 197.7 %reduce-scatter.31.cloned.1.call-done = f32[64,4608]{1,0:T(8,128)} async-done(((f32[1024,4608]{1,0:T(8,128)}), f32[64,4608]{1,0:T(8,128)}) %reduce-scatter.31.cloned.1.call-update) | async-done | bytes 1179664 | tf_op jit(solution)/shard_map/reduce_scatter | solution.py:41
  866.8 197.8 %reduce-scatter.35.cloned.1.call-done = f32[64,4608]{1,0:T(8,128)} async-done(((f32[1024,4608]{1,0:T(8,128)}), f32[64,4608]{1,0:T(8,128)}) %reduce-scatter.35.cloned.1.call-update) | async-done | bytes 1179664 | tf_op jit(solution)/shard_map/reduce_scatter | solution.py:41
  1064.7 198.1 %reduce-scatter.39.cloned.1.call-done = f32[288,1024]{1,0:T(8,128)} async-done(((f32[4608,1024]{1,0:T(8,128)}), f32[288,1024]{1,0:T(8,128)}) %reduce-scatter.39.cloned.1.call-update) | async-done | bytes 1179664 | tf_op jit(solution)/shard_map/reduce_scatter | solution.py:41
  1262.9 10.1 add_bitcast_fusion
  1278.8 39.5 %all-reduce = (f32[1024]{0:T(1024)}, f32[64]{0:T(128)}, f32[64]{0:T(128)}, f32[1024]{0:T(1024)}) all-reduce(f32[1024]{0:T(1024)S(1)} %get-tuple-element.190, f32[64]{0:T(128)S(1)} %get-tuple-element.186, f32[64]{0:T(128)S(1)} %get-tuple-element.192, f32[1024]{0:T(1024)S(1)} %copy-done.46), channel_id=1, replica_groups=mesh['dp'=16,'seq'=2] {'dp','seq'}, use_global_device_ids=true, to_apply=%region_18.19 | all-reduce | flops 2176 | bytes 17408 | tf_op jit(solution)/shard_map/psum | solution.py:211
  1322.6 19.4 %reduce-scatter.33.cloned.1.call-done = f32[64,2304]{1,0:T(8,128)} async-done(((f32[64,4608]{1,0:T(8,128)}), f32[64,2304]{1,0:T(8,128)}) %reduce-scatter.33.cloned.1.call-update) | async-done | bytes 589840 | tf_op jit(solution)/shard_map/reduce_scatter | solution.py:42
  1342.0 24.7 %reduce-scatter.37.cloned.1.call-done = f32[64,2304]{1,0:T(8,128)} async-done(((f32[64,4608]{1,0:T(8,128)}), f32[64,2304]{1,0:T(8,128)}) %reduce-scatter.37.cloned.1.call-update) | async-done | bytes 589840 | tf_op jit(solution)/shard_map/reduce_scatter | solution.py:42
  1366.7 24.4 %reduce-scatter.41.cloned.1.call-done = f32[288,512]{1,0:T(8,128)} async-done(((f32[288,1024]{1,0:T(8,128)}), f32[288,512]{1,0:T(8,128)}) %reduce-scatter.41.cloned.1.call-update) | async-done | bytes 589840 | tf_op jit(solution)/shard_map/reduce_scatter | solution.py:42
  (239 shorter events, 108.6 us)
Async XLA Ops:
  7.2 126.6 %copy-start = (bf16[1024,1024]{1,0:T(8,128)(2,1)S(1)}, bf16[1024,1024]{1,0:T(8,128)(2,1)}, u32[]{:S(2)}) copy-start(bf16[1024,1024]{1,0:T(8,128)(2,1)} %param.27) | copy-start | bytes 6291460
  7.2 4.7 copy-start.2
  8.9 19.1 %copy-start.40 = (f32[512]{0:T(512)}, f32[512]{0:T(512)S(1)}, u32[]{:S(2)}) copy-start(f32[512]{0:T(512)S(1)} %add_rsqrt_fusion.3) | copy-start | bytes 6148
  9.6 18.4 %copy-start.38 = (f32[1024]{0:T(1024)}, f32[1024]{0:T(1024)S(1)}, u32[]{:S(2)}) copy-start(f32[1024]{0:T(1024)S(1)} %convert_element_type.137) | copy-start | bytes 12292
  11.9 3.1 copy-start.49
  14.9 3.4 copy-start.36
  15.0 3.4 copy-start.44
  15.0 3.1 copy-start.16
  18.1 13.4 copy-start.24
  19.7 19.6 %all-to-all-start.1 = ((bf16[512,8,128]{0,2,1:T(8,128)(2,1)}), bf16[512,8,128]{0,2,1:T(8,128)(2,1)}, u32[]{:S(2)}, u32[]{:S(2)}) async-start(bf16[512,8,128]{0,2,1:T(8,128)(2,1)} %pad_maximum_fusion.2), calls=%async_computation.1 | async-start | bytes 2097152 | tf_op jit(solution)/shard_map/all_to_all | solution.py:96
  28.0 3.0 copy-start.50
  32.7 11.2 copy-start.51
  39.2 18.0 %all-to-all-start = ((bf16[512,8,128]{0,2,1:T(8,128)(2,1)}), bf16[512,8,128]{0,2,1:T(8,128)(2,1)}, u32[]{:S(2)}, u32[]{:S(2)}) async-start(bf16[512,8,128]{0,2,1:T(8,128)(2,1)} %bitcast.7), calls=%async_computation | async-start | bytes 2097152 | tf_op jit(solution)/shard_map/all_to_all | solution.py:95
  100.6 11.2 copy-start.5
  100.6 11.2 copy-start.34
  106.7 10.0 copy-start.47
  111.8 17.3 %all-to-all-start.2 = ((bf16[1024,4,128]{2,1,0:T(4,128)(2,1)}), bf16[1024,4,128]{2,1,0:T(4,128)(2,1)}, u32[]{:S(2)}, u32[]{:S(2)}) async-start(bf16[1024,4,128]{2,1,0:T(4,128)(2,1)} %reshape.352), calls=%async_computation.2 | async-start | bytes 2097152 | tf_op jit(solution)/shard_map/all_to_all | solution.py:129
  116.7 17.1 %copy-start.3 = (bf16[1,512,1024]{2,1,0:T(8,128)(2,1)S(1)}, bf16[1,512,1024]{2,1,0:T(8,128)(2,1)}, u32[]{:S(2)}) copy-start(bf16[1,512,1024]{2,1,0:T(8,128)(2,1)} %param.18) | copy-start | bytes 3145732
  133.8 4.6 copy-start.48
  137.8 8.1 slice-start
  138.4 7.6 copy-start.14
  138.4 7.6 slice-start.1
  138.4 7.6 slice-start.2
  146.0 7.4 copy-start.27
  173.8 9.2 copy-start.12
  173.8 9.2 copy-start.21
  194.9 15.1 %all-to-all-start.3 = ((bf16[512,8,128]{2,0,1:T(8,128)(2,1)}), bf16[512,8,128]{2,0,1:T(8,128)(2,1)S(1)}, u32[]{:S(2)}, u32[]{:S(2)}) async-start(bf16[512,8,128]{2,0,1:T(8,128)(2,1)} %bitcast.254), calls=%async_computation.3 | async-start | bytes 2097152 | tf_op jit(solution)/shard_map/all_to_all | solution.py:159
  198.5 268.9 %reduce-scatter.19.cloned.1.call-start = ((), (), s32[]{:S(2)}) async-start(), calls=%async_computation.22 | async-start | bytes 2228224 | tf_op jit(solution)/shard_map/reduce_scatter | solution.py:41
  212.0 3.0 copy-start.6
  212.0 3.0 copy-start.35
  391.5 125.9 %reduce-scatter.23.cloned.1.call-start = ((), (), s32[]{:S(2)}) async-start(), calls=%async_computation.24 | async-start | bytes 2228224 | tf_op jit(solution)/shard_map/reduce_scatter | solution.py:41
  391.5 3.6 copy-start.10
  395.1 197.9 %reduce-scatter.27.cloned.1.call-start = ((), (), s32[]{:S(2)}) async-start(), calls=%async_computation.26 | async-start | bytes 4456448 | tf_op jit(solution)/shard_map/reduce_scatter | solution.py:41
  399.7 269.3 %reduce-scatter.15.cloned.1.call-start = ((), (), s32[]{:S(2)}) async-start(), calls=%async_computation.20 | async-start | bytes 4456448 | tf_op jit(solution)/shard_map/reduce_scatter | solution.py:41
  429.7 437.0 %reduce-scatter.31.cloned.1.call-start = ((), (), s32[]{:S(2)}) async-start(), calls=%async_computation.28 | async-start | bytes 20054016 | tf_op jit(solution)/shard_map/reduce_scatter | solution.py:41
  442.5 622.1 %reduce-scatter.35.cloned.1.call-start = ((), (), s32[]{:S(2)}) async-start(), calls=%async_computation.30 | async-start | bytes 20054016 | tf_op jit(solution)/shard_map/reduce_scatter | solution.py:41
  454.4 808.4 %reduce-scatter.39.cloned.1.call-start = ((), (), s32[]{:S(2)}) async-start(), calls=%async_computation.32 | async-start | bytes 20054016 | tf_op jit(solution)/shard_map/reduce_scatter | solution.py:41
  467.3 855.2 %reduce-scatter.21.cloned.1.call-start = ((), (), s32[]{:S(2)}) async-start(), calls=%async_computation.23 | async-start | bytes 196608 | tf_op jit(solution)/shard_map/reduce_scatter | solution.py:42
  468.1 854.5 %reduce-scatter.25.cloned.1.call-start = ((), (), s32[]{:S(2)}) async-start(), calls=%async_computation.25 | async-start | bytes 196608 | tf_op jit(solution)/shard_map/reduce_scatter | solution.py:42
  517.4 745.5 %copy-start.13 = (f32[512,1024]{1,0:T(8,128)S(1)}, f32[512,1024]{1,0:T(8,128)}, u32[]{:S(2)}) copy-start(f32[512,1024]{1,0:T(8,128)} %copy-done.11) | copy-start | bytes 6291460
  517.4 805.2 %reduce-scatter.29.cloned.1.call-start = ((), (), s32[]{:S(2)}) async-start(), calls=%async_computation.27 | async-start | bytes 393216 | tf_op jit(solution)/shard_map/reduce_scatter | solution.py:42
  593.0 729.5 %reduce-scatter.17.cloned.1.call-start = ((), (), s32[]{:S(2)}) async-start(), calls=%async_computation.21 | async-start | bytes 393216 | tf_op jit(solution)/shard_map/reduce_scatter | solution.py:42
  669.0 672.9 %reduce-scatter.33.cloned.1.call-start = ((), (), s32[]{:S(2)}) async-start(), calls=%async_computation.29 | async-start | bytes 1769472 | tf_op jit(solution)/shard_map/reduce_scatter | solution.py:42
  866.8 499.9 %reduce-scatter.37.cloned.1.call-start = ((), (), s32[]{:S(2)}) async-start(), calls=%async_computation.31 | async-start | bytes 1769472 | tf_op jit(solution)/shard_map/reduce_scatter | solution.py:42
  1064.6 326.5 %reduce-scatter.41.cloned.1.call-start = ((), (), s32[]{:S(2)}) async-start(), calls=%async_computation.33 | async-start | bytes 1769472 | tf_op jit(solution)/shard_map/reduce_scatter | solution.py:42
  1262.9 10.1 copy-start.20
  1262.9 10.1 copy-start.22
  1318.3 72.8 %copy-start.1 = (bf16[1024,1024]{1,0:T(8,128)(2,1)S(1)}, bf16[1024,1024]{1,0:T(8,128)(2,1)}, u32[]{:S(2)}) copy-start(bf16[1024,1024]{1,0:T(8,128)(2,1)} %param.27) | copy-start | bytes 6291460
  (25 other events, 39.6 us)
Sparse Core Ops, SparseCore 0:
  391.6 60.9 reduce-scatter.18
  456.8 60.5 reduce-scatter.22
  521.2 71.7 reduce-scatter.26
  597.2 71.7 reduce-scatter.14
  673.0 193.7 reduce-scatter.30
  870.7 193.8 reduce-scatter.34
  1068.7 194.0 reduce-scatter.38
  1265.6 9.3 reduce-scatter.20
  1277.8 10.5 reduce-scatter.24
  1291.1 11.3 reduce-scatter.28
  1305.3 11.8 reduce-scatter.16
  1319.8 22.0 reduce-scatter.32
  1344.9 21.7 reduce-scatter.36
  1369.4 21.7 reduce-scatter.40
where the time goes:
time: 1400 us
  waiting for transfers between devices  901 us (64%)
  matrix products  297 us (21%)
  blocking collectives  65.9 us (5%)
  local copies, waits for them, and re-layouts  60.8 us (4%)
  other arithmetic  32.4 us (2%)
  starting transfers between devices  18 us (1%)
  between operations  15.1 us (1%)
    reduce_scatter x7, waiting for transfers between devices, reduce_grads(): partial_sum = lax.psum_scatter(grads, 'dp', scatter_dimension=0, tiled=True)  794 us
    reduce_scatter x7, waiting for transfers between devices, reduce_grads(): return lax.psum_scatter(partial_sum, 'seq', scatter_dimension=1, tiled=True)  68.6 us
    dot_general x2, matrix products, attend_back(): jnp.einsum('hgqk,khd->qhgd', d_scores, key_all, preferred_element_type=f32)  50.9 us
    dot_general x2, matrix products, attend_back(): jnp.einsum('hgqk,qhgd->khd', d_scores, query_block, preferred_element_typ...  46 us
    psum x1, blocking collectives, body(): lax.psum((jnp.sum(attn_gain_terms, axis=0), jnp.sum(query_gain_terms, axi...  39.5 us
  transfers between devices with their start and end apart: 18, of which 13 were waited for; matrix products, arithmetic and copies ran while one was open for 6% of the time, Pallas kernels for 0%

commit v1 on v0

--- a/solution.py
+++ b/solution.py
@@ -208,15 +208,14 @@
     d_input_norm, attn_gain_terms = norm_back(d_normed, inputs, gain_attn)
     d_inputs = d_hidden + d_input_norm
     attn_sums = reduce_grads((grad_query, grad_key, grad_value, grad_out))
-    gain_totals = lax.psum(
-        (
-            jnp.sum(attn_gain_terms, axis=0),
-            jnp.sum(query_gain_terms, axis=(0, 1)),
-            jnp.sum(key_gain_terms, axis=(0, 1)),
-            jnp.sum(ffn_gain_terms, axis=0),
-        ),
-        ("dp", "seq"),
-    )
+    gain_totals = (
+        jnp.sum(attn_gain_terms, axis=0),
+        jnp.sum(query_gain_terms, axis=(0, 1)),
+        jnp.sum(key_gain_terms, axis=(0, 1)),
+        jnp.sum(ffn_gain_terms, axis=0),
+    )
+    for over in ("dp", "seq"):
+        gain_totals = lax.psum(gain_totals, over)
     return (
         output[None],
         d_inputs[None],

time: 1400 us -> 1400 us (level)
    psum x1 -> x2, blocking collectives: 39.5 us -> 38.2 us  [body(): gain_totals = lax.psum(gain_totals, over)]
where the time goes in v1:
time: 1400 us
  waiting for transfers between devices  902 us (64%)
  matrix products  297 us (21%)
  blocking collectives  64.5 us (5%)
  local copies, waits for them, and re-layouts  60.7 us (4%)
  other arithmetic  32.5 us (2%)
  starting transfers between devices  18 us (1%)
  between operations  15.1 us (1%)
    reduce_scatter x7, waiting for transfers between devices, reduce_grads(): partial_sum = lax.psum_scatter(grads, 'dp', scatter_dimension=0, tiled=True)  795 us
    reduce_scatter x7, waiting for transfers between devices, reduce_grads(): return lax.psum_scatter(partial_sum, 'seq', scatter_dimension=1, tiled=True)  69.4 us
    dot_general x2, matrix products, attend_back(): jnp.einsum('hgqk,khd->qhgd', d_scores, key_all, preferred_element_type=f32)  51 us
    dot_general x2, matrix products, attend_back(): jnp.einsum('hgqk,qhgd->khd', d_scores, query_block, preferred_element_typ...  46 us
    psum x2, blocking collectives, body(): gain_totals = lax.psum(gain_totals, over)  38.2 us
  transfers between devices with their start and end apart: 18, of which 13 were waited for; matrix products, arithmetic and copies ran while one was open for 6% of the time, Pallas kernels for 0%

profile of v1, /device:TPU:0, one launch (start us, length us, event | category | flops | bytes accessed | tf_op | source)
XLA Modules:
  0.0 1397.9 jit_solution(13141782732980944463)
XLA Ops:
  19.7 4.4 all-to-all-start.1
  33.8 5.5 all-to-all-done.1
  39.2 4.6 all-to-all-start
  49.3 7.9 all-to-all-done
  64.2 36.4 %while.28 = (s32[]{:T(128)}, bf16[2,512,4,2,64]{1,4,3,2,0:T(8,128)(2,1)}, f32[2,4,2,512]{3,2,1,0:T(2,128)S(1)}, s32[2]{0:T(128)S(1)}, s32[1024]{0:T(1024)S(1)}, ...) while((s32[]{:T(128)}, ...), condition=%wide.region_8.9_spmd.clone, body=%wide.region_5.8_spmd.clone.sunk | while | flops 1125904896 | bytes 54672044 | solution.py:127
  68.0 4.4 bitcast_reduce_fusion.2
  76.8 5.6 fusion.162
  95.0 5.6 fusion.162
  100.6 6.1 copy.115
  106.7 5.1 reshape.352
  111.8 4.8 all-to-all-start.2
  116.7 12.4 all-to-all-done.2
  138.3 7.5 fusion.102
  145.8 7.5 fusion.103
  153.3 20.4 %multiply_convert_fusion = (bf16[512,4608]{1,0:T(8,128)(2,1)}, bf16[512,4608]{1,0:T(8,128)(2,1)}, bf16[512,4608]{1,0:T(8,128)(2,1)}) fusion(f32[512,4608]{1,0:T(8,128)} %fusion.102, f32[512,4608]{1,0:T(8,128)} %fusion.103, bf16[4608,1024]{1,0:T(8,128)(2,1)} %param.31, bf16[1,512,1024]{2,1,0:T(8,128)(2,1)S(1)} %copy-done.27), kind=kOutput, calls=%fused_computation.63 | convolution fusion | flops 4869586944 | bytes 43515904 | tf_op jit(solution)/shard_map/td,fd->tf/dot_general | solution.py:140
  173.7 9.2 fusion.104
  182.9 8.8 multiply_reduce_fusion
  198.5 11.4 all-to-all-done.3
  214.9 155.5 %while.29 = (s32[]{:T(128)}, f32[1024,4,64]{0,2,1:T(8,128)}, f32[1024,4,64]{0,2,1:T(8,128)S(1)}, bf16[2,512,4,2,64]{1,4,3,2,0:T(8,128)(2,1)}, s32[2]{0:T(128)S(1...) while((s32[]{:T(128)}, f32[1024,4,64]{0,2,1:T(8,128)}, ...), condition=%wide.region_13.14_spmd.clone, body=%wide.region_11.13_spmd.clone.sunk | while | flops 2745969152 | bytes 194050784 | solution.py:186
  218.8 9.6 fusion.172
  228.3 8.2 fusion.173
  236.5 25.5 %fusion.176 = bf16[2,512,4,2,64]{1,4,3,2,0:T(8,128)(2,1)} fusion(bf16[2,512,4,2,64]{1,4,3,2,0:T(8,128)(2,1)} %get-tuple-element.438, s32[]{:T(128)} %get-tuple-element.435, f32[4,2,512,1024]{3,2,1,0:T(8,128)} %fusion.172, f32[4,512,2,1024]{3,1,2,0:T(8,128)} %fusion.173, bf16[1024,4,64]{0,2,1:T(8,128)(2,1)S(1)} %get-tuple-element.456), kind=kOutput, calls=%fused_computation.44.clone.1 | convolution fusion | flops 558109696 | bytes 68157952 | tf_op jit(solution)/shard_map/while/body/eval_jaxpr/hgqk,khd->qhgd/dot_general | solution.py:176
  262.1 22.8 %fusion.174 = f32[1024,4,64]{0,2,1:T(8,128)} fusion(f32[4,2,512,1024]{3,2,1,0:T(8,128)} %fusion.172, f32[4,512,2,1024]{3,1,2,0:T(8,128)} %fusion.173, f32[1024,4,64]{0,2,1:T(8,128)} %get-tuple-element.436, pred[]{:T(512)S(6)} %compare.3, bf16[1024,4,2,64]{0,3,2,1:T(8,128)(2,1)} %get-tuple-element.454, s32[]{:T(128)S(6)} %select_n.56), kind=kOutput, calls=%fused_computation.39.clone.1 | convolution fusion | flops 558371840 | bytes 69730312 | tf_op jit(solution)/shard_map/while/body/eval_jaxpr/hgqk,qhgd->khd/dot_general | solution.py:177
  284.9 7.6 fusion.175
  296.3 9.6 fusion.172
  305.9 8.2 fusion.173
  314.1 25.5 %fusion.176 = bf16[2,512,4,2,64]{1,4,3,2,0:T(8,128)(2,1)} fusion(bf16[2,512,4,2,64]{1,4,3,2,0:T(8,128)(2,1)} %get-tuple-element.438, s32[]{:T(128)} %get-tuple-element.435, f32[4,2,512,1024]{3,2,1,0:T(8,128)} %fusion.172, f32[4,512,2,1024]{3,1,2,0:T(8,128)} %fusion.173, bf16[1024,4,64]{0,2,1:T(8,128)(2,1)S(1)} %get-tuple-element.456), kind=kOutput, calls=%fused_computation.44.clone.1 | convolution fusion | flops 558109696 | bytes 68157952 | tf_op jit(solution)/shard_map/while/body/eval_jaxpr/hgqk,khd->qhgd/dot_general | solution.py:176
  339.6 23.2 %fusion.174 = f32[1024,4,64]{0,2,1:T(8,128)} fusion(f32[4,2,512,1024]{3,2,1,0:T(8,128)} %fusion.172, f32[4,512,2,1024]{3,1,2,0:T(8,128)} %fusion.173, f32[1024,4,64]{0,2,1:T(8,128)} %get-tuple-element.436, pred[]{:T(512)S(6)} %compare.3, bf16[1024,4,2,64]{0,3,2,1:T(8,128)(2,1)} %get-tuple-element.454, s32[]{:T(128)S(6)} %select_n.56), kind=kOutput, calls=%fused_computation.39.clone.1 | convolution fusion | flops 558371840 | bytes 69730312 | tf_op jit(solution)/shard_map/while/body/eval_jaxpr/hgqk,qhgd->khd/dot_general | solution.py:177
  362.8 7.6 fusion.175
  372.6 13.2 all_to_all.90
  395.1 4.5 fusion.91
  399.7 4.6 copy.116
  406.1 13.2 all_to_all.91
  430.9 11.6 fusion.107
  442.5 11.8 fusion.108
  455.6 11.7 fusion.75
  468.1 49.3 %reduce-scatter.23.cloned.1.call-done = f32[64,512]{1,0:T(8,128)} async-done(((f32[1024,512]{1,0:T(8,128)}), f32[64,512]{1,0:T(8,128)}) %reduce-scatter.23.cloned.1.call-update) | async-done | bytes 131088 | tf_op jit(solution)/shard_map/reduce_scatter | solution.py:41
  517.5 75.5 %reduce-scatter.27.cloned.1.call-done = f32[64,1024]{1,0:T(8,128)} async-done(((f32[1024,1024]{1,0:T(8,128)}), f32[64,1024]{1,0:T(8,128)}) %reduce-scatter.27.cloned.1.call-update) | async-done | bytes 262160 | tf_op jit(solution)/shard_map/reduce_scatter | solution.py:41
  593.0 76.1 %reduce-scatter.15.cloned.1.call-done = f32[64,1024]{1,0:T(8,128)} async-done(((f32[1024,1024]{1,0:T(8,128)}), f32[64,1024]{1,0:T(8,128)}) %reduce-scatter.15.cloned.1.call-update) | async-done | bytes 262160 | tf_op jit(solution)/shard_map/reduce_scatter | solution.py:41
  669.1 197.8 %reduce-scatter.31.cloned.1.call-done = f32[64,4608]{1,0:T(8,128)} async-done(((f32[1024,4608]{1,0:T(8,128)}), f32[64,4608]{1,0:T(8,128)}) %reduce-scatter.31.cloned.1.call-update) | async-done | bytes 1179664 | tf_op jit(solution)/shard_map/reduce_scatter | solution.py:41
  867.1 197.9 %reduce-scatter.35.cloned.1.call-done = f32[64,4608]{1,0:T(8,128)} async-done(((f32[1024,4608]{1,0:T(8,128)}), f32[64,4608]{1,0:T(8,128)}) %reduce-scatter.35.cloned.1.call-update) | async-done | bytes 1179664 | tf_op jit(solution)/shard_map/reduce_scatter | solution.py:41
  1065.1 198.1 %reduce-scatter.39.cloned.1.call-done = f32[288,1024]{1,0:T(8,128)} async-done(((f32[4608,1024]{1,0:T(8,128)}), f32[288,1024]{1,0:T(8,128)}) %reduce-scatter.39.cloned.1.call-update) | async-done | bytes 1179664 | tf_op jit(solution)/shard_map/reduce_scatter | solution.py:41
  1263.2 10.1 add_bitcast_fusion
  1279.1 32.5 %all-reduce = (f32[1024]{0:T(1024)S(1)}, f32[64]{0:T(128)S(1)}, f32[64]{0:T(128)S(1)}, f32[1024]{0:T(1024)S(1)}) all-reduce(f32[1024]{0:T(1024)S(1)} %get-tuple-element.190, f32[64]{0:T(128)S(1)} %get-tuple-element.186, f32[64]{0:T(128)S(1)} %get-tuple-element.192, f32[1024]{0:T(1024)S(1)} %copy-done.46), channel_id=1, replica_groups=mesh['dp'=16,'seq'=2] {'dp'}, use_global_device_ids=true, to_apply=%region_18.19 | all-reduce | flops 2176 | bytes 17408 | tf_op jit(solution)/shard_map/psum | solution.py:218
  1311.6 5.7 all-reduce.1
  1321.5 20.3 %reduce-scatter.33.cloned.1.call-done = f32[64,2304]{1,0:T(8,128)} async-done(((f32[64,4608]{1,0:T(8,128)}), f32[64,2304]{1,0:T(8,128)}) %reduce-scatter.33.cloned.1.call-update) | async-done | bytes 589840 | tf_op jit(solution)/shard_map/reduce_scatter | solution.py:42
  1341.8 24.7 %reduce-scatter.37.cloned.1.call-done = f32[64,2304]{1,0:T(8,128)} async-done(((f32[64,4608]{1,0:T(8,128)}), f32[64,2304]{1,0:T(8,128)}) %reduce-scatter.37.cloned.1.call-update) | async-done | bytes 589840 | tf_op jit(solution)/shard_map/reduce_scatter | solution.py:42
  1366.5 24.4 %reduce-scatter.41.cloned.1.call-done = f32[288,512]{1,0:T(8,128)} async-done(((f32[288,1024]{1,0:T(8,128)}), f32[288,512]{1,0:T(8,128)}) %reduce-scatter.41.cloned.1.call-update) | async-done | bytes 589840 | tf_op jit(solution)/shard_map/reduce_scatter | solution.py:42
  (240 shorter events, 112.9 us)
Async XLA Ops:
  7.2 126.6 %copy-start = (bf16[1024,1024]{1,0:T(8,128)(2,1)S(1)}, bf16[1024,1024]{1,0:T(8,128)(2,1)}, u32[]{:S(2)}) copy-start(bf16[1024,1024]{1,0:T(8,128)(2,1)} %param.27) | copy-start | bytes 6291460
  7.2 4.7 copy-start.2
  8.9 19.2 %copy-start.40 = (f32[512]{0:T(512)}, f32[512]{0:T(512)S(1)}, u32[]{:S(2)}) copy-start(f32[512]{0:T(512)S(1)} %add_rsqrt_fusion.3) | copy-start | bytes 6148
  9.6 18.5 %copy-start.38 = (f32[1024]{0:T(1024)}, f32[1024]{0:T(1024)S(1)}, u32[]{:S(2)}) copy-start(f32[1024]{0:T(1024)S(1)} %convert_element_type.137) | copy-start | bytes 12292
  11.9 3.1 copy-start.49
  15.0 3.4 copy-start.36
  15.0 3.4 copy-start.44
  15.0 3.1 copy-start.16
  18.1 13.5 copy-start.24
  19.7 19.6 %all-to-all-start.1 = ((bf16[512,8,128]{0,2,1:T(8,128)(2,1)}), bf16[512,8,128]{0,2,1:T(8,128)(2,1)}, u32[]{:S(2)}, u32[]{:S(2)}) async-start(bf16[512,8,128]{0,2,1:T(8,128)(2,1)} %pad_maximum_fusion.2), calls=%async_computation.1 | async-start | bytes 2097152 | tf_op jit(solution)/shard_map/all_to_all | solution.py:96
  28.1 3.0 copy-start.50
  32.7 11.2 copy-start.51
  39.2 18.0 %all-to-all-start = ((bf16[512,8,128]{0,2,1:T(8,128)(2,1)}), bf16[512,8,128]{0,2,1:T(8,128)(2,1)}, u32[]{:S(2)}, u32[]{:S(2)}) async-start(bf16[512,8,128]{0,2,1:T(8,128)(2,1)} %bitcast.7), calls=%async_computation | async-start | bytes 2097152 | tf_op jit(solution)/shard_map/all_to_all | solution.py:95
  100.6 11.2 copy-start.5
  100.6 11.2 copy-start.34
  106.7 10.0 copy-start.47
  111.8 17.3 %all-to-all-start.2 = ((bf16[1024,4,128]{2,1,0:T(4,128)(2,1)}), bf16[1024,4,128]{2,1,0:T(4,128)(2,1)}, u32[]{:S(2)}, u32[]{:S(2)}) async-start(bf16[1024,4,128]{2,1,0:T(4,128)(2,1)} %reshape.352), calls=%async_computation.2 | async-start | bytes 2097152 | tf_op jit(solution)/shard_map/all_to_all | solution.py:129
  116.7 17.1 %copy-start.3 = (bf16[1,512,1024]{2,1,0:T(8,128)(2,1)S(1)}, bf16[1,512,1024]{2,1,0:T(8,128)(2,1)}, u32[]{:S(2)}) copy-start(bf16[1,512,1024]{2,1,0:T(8,128)(2,1)} %param.18) | copy-start | bytes 3145732
  133.8 4.6 copy-start.48
  137.8 8.0 slice-start
  138.3 7.5 copy-start.14
  138.3 7.5 slice-start.1
  138.3 7.5 slice-start.2
  145.8 7.5 copy-start.27
  173.7 9.2 copy-start.12
  173.7 9.2 copy-start.21
  194.9 15.0 %all-to-all-start.3 = ((bf16[512,8,128]{2,0,1:T(8,128)(2,1)}), bf16[512,8,128]{2,0,1:T(8,128)(2,1)S(1)}, u32[]{:S(2)}, u32[]{:S(2)}) async-start(bf16[512,8,128]{2,0,1:T(8,128)(2,1)} %bitcast.254), calls=%async_computation.3 | async-start | bytes 2097152 | tf_op jit(solution)/shard_map/all_to_all | solution.py:159
  198.4 268.9 %reduce-scatter.19.cloned.1.call-start = ((), (), s32[]{:S(2)}) async-start(), calls=%async_computation.22 | async-start | bytes 2228224 | tf_op jit(solution)/shard_map/reduce_scatter | solution.py:41
  211.9 3.0 copy-start.6
  211.9 3.0 copy-start.35
  391.5 125.9 %reduce-scatter.23.cloned.1.call-start = ((), (), s32[]{:S(2)}) async-start(), calls=%async_computation.24 | async-start | bytes 2228224 | tf_op jit(solution)/shard_map/reduce_scatter | solution.py:41
  391.5 3.6 copy-start.10
  395.1 197.9 %reduce-scatter.27.cloned.1.call-start = ((), (), s32[]{:S(2)}) async-start(), calls=%async_computation.26 | async-start | bytes 4456448 | tf_op jit(solution)/shard_map/reduce_scatter | solution.py:41
  399.7 269.4 %reduce-scatter.15.cloned.1.call-start = ((), (), s32[]{:S(2)}) async-start(), calls=%async_computation.20 | async-start | bytes 4456448 | tf_op jit(solution)/shard_map/reduce_scatter | solution.py:41
  429.7 437.3 %reduce-scatter.31.cloned.1.call-start = ((), (), s32[]{:S(2)}) async-start(), calls=%async_computation.28 | async-start | bytes 20054016 | tf_op jit(solution)/shard_map/reduce_scatter | solution.py:41
  442.5 622.5 %reduce-scatter.35.cloned.1.call-start = ((), (), s32[]{:S(2)}) async-start(), calls=%async_computation.30 | async-start | bytes 20054016 | tf_op jit(solution)/shard_map/reduce_scatter | solution.py:41
  454.4 808.8 %reduce-scatter.39.cloned.1.call-start = ((), (), s32[]{:S(2)}) async-start(), calls=%async_computation.32 | async-start | bytes 20054016 | tf_op jit(solution)/shard_map/reduce_scatter | solution.py:41
  467.3 854.2 %reduce-scatter.21.cloned.1.call-start = ((), (), s32[]{:S(2)}) async-start(), calls=%async_computation.23 | async-start | bytes 196608 | tf_op jit(solution)/shard_map/reduce_scatter | solution.py:42
  468.0 853.5 %reduce-scatter.25.cloned.1.call-start = ((), (), s32[]{:S(2)}) async-start(), calls=%async_computation.25 | async-start | bytes 196608 | tf_op jit(solution)/shard_map/reduce_scatter | solution.py:42
  517.4 745.8 %copy-start.13 = (f32[512,1024]{1,0:T(8,128)S(1)}, f32[512,1024]{1,0:T(8,128)}, u32[]{:S(2)}) copy-start(f32[512,1024]{1,0:T(8,128)} %copy-done.11) | copy-start | bytes 6291460
  517.4 804.1 %reduce-scatter.29.cloned.1.call-start = ((), (), s32[]{:S(2)}) async-start(), calls=%async_computation.27 | async-start | bytes 393216 | tf_op jit(solution)/shard_map/reduce_scatter | solution.py:42
  592.9 728.6 %reduce-scatter.17.cloned.1.call-start = ((), (), s32[]{:S(2)}) async-start(), calls=%async_computation.21 | async-start | bytes 393216 | tf_op jit(solution)/shard_map/reduce_scatter | solution.py:42
  669.1 672.7 %reduce-scatter.33.cloned.1.call-start = ((), (), s32[]{:S(2)}) async-start(), calls=%async_computation.29 | async-start | bytes 1769472 | tf_op jit(solution)/shard_map/reduce_scatter | solution.py:42
  867.0 499.5 %reduce-scatter.37.cloned.1.call-start = ((), (), s32[]{:S(2)}) async-start(), calls=%async_computation.31 | async-start | bytes 1769472 | tf_op jit(solution)/shard_map/reduce_scatter | solution.py:42
  1065.0 325.9 %reduce-scatter.41.cloned.1.call-start = ((), (), s32[]{:S(2)}) async-start(), calls=%async_computation.33 | async-start | bytes 1769472 | tf_op jit(solution)/shard_map/reduce_scatter | solution.py:42
  1263.2 10.1 copy-start.20
  1263.2 10.1 copy-start.22
  1317.3 73.7 %copy-start.1 = (bf16[1024,1024]{1,0:T(8,128)(2,1)S(1)}, bf16[1024,1024]{1,0:T(8,128)(2,1)}, u32[]{:S(2)}) copy-start(bf16[1024,1024]{1,0:T(8,128)(2,1)} %param.27) | copy-start | bytes 6291460
  (25 other events, 39.6 us)
Sparse Core Ops, SparseCore 0:
  391.6 60.9 reduce-scatter.18
  456.8 60.5 reduce-scatter.22
  521.3 71.6 reduce-scatter.26
  597.1 71.9 reduce-scatter.14
  673.0 193.9 reduce-scatter.30
  871.0 193.9 reduce-scatter.34
  1069.1 193.9 reduce-scatter.38
  1265.9 9.3 reduce-scatter.20
  1278.1 10.2 reduce-scatter.24
  1291.0 11.6 reduce-scatter.28
  1305.6 11.6 reduce-scatter.16
  1320.0 21.7 reduce-scatter.32
  1344.7 21.7 reduce-scatter.36
  1369.2 21.7 reduce-scatter.40
